TPU v7x, 256 devices: a whole 4x4x8 slice. The times are simulated.
256 devices in a mesh: mp: 4 (over z_lo, core), fsdp: 16 (over y, x), dp: 4 (over z_hi).
Axes of the slice: x: 4, y: 4, z: 8 (z_hi: 4, z_lo: 2; z = z_hi * 2 + z_lo), core: 2. Of those that a mesh axis runs over, the one named last changes fastest.
Arguments:
- gen_noise: float32 [4, 4096, 128], P('dp', 'fsdp'), may hold values from -6 to 6
- renoise: float32 [4, 4096, 128], P('dp', 'fsdp'), may hold values from -120 to 120
- gen_step: int32 [4], P('dp'), may hold values from 250 to 999
- renoise_step: int32 [4], P('dp'), may hold values from 20 to 979
- text_pooled: bfloat16 [4, 768], P('dp'), may hold values from -6 to 6
- embed: bfloat16 [3, 64, 3072], replicated, may hold values from -0.75 to 0.75
- mod_weight: bfloat16 [3, 1024, 6144], P(None, None, 'fsdp'), may hold values from -0.1875 to 0.1875
- proj_weight: bfloat16 [3, 3072, 3072], P(None, 'fsdp', 'mp'), may hold values from -0.109375 to 0.109375
- unembed: bfloat16 [3, 64, 3072], P(None, None, 'mp'), may hold values from -0.109375 to 0.109375
Outputs:
- gen_grad: float32 [3072, 3072], P('fsdp', 'mp')
- score_gap: float32 [4, 4096, 128], P('dp', 'fsdp')
All inputs are finite; a program needn't handle non-finite values. Where the computation divides by a largest or mean magnitude, that divisor is 1e-20 or more.
Results may differ from a plain program's by a relative error of at most 0.03.
Values may be sent and summed in bfloat16 or wider, within the bound.
A program may use at most 128 MiB of HBM per device.

v0:
```python
import math
import jax
import jax.numpy as jnp
from jax import lax
from jax.sharding import PartitionSpec as P

D = 3072
CH = 64
TEMB = 256
GUIDANCE = 3.5
EPS_NORM = 1e-06
EPS_GAP = 1e-05
HIGH = lax.Precision.HIGHEST


def sinusoid(timesteps):
    half_size = TEMB // 2
    frequency = jnp.exp(-math.log(10000.0) * jnp.arange(half_size, dtype=jnp.float32) / half_size)
    angles = timesteps.astype(jnp.float32)[:, None] * frequency[None, :]
    return jnp.concatenate([jnp.cos(angles), jnp.sin(angles)], axis=1)


def condition(timesteps, pooled):
    joined = jnp.concatenate([sinusoid(timesteps), pooled.astype(jnp.float32)], axis=1)
    return jax.nn.silu(joined).astype(jnp.bfloat16)


def mm(left, right):
    return jnp.dot(left, right, precision=HIGH, preferred_element_type=jnp.float32)


def doubled(block):
    zero = jnp.zeros_like(block)
    return jnp.concatenate(
        [jnp.concatenate([block, zero], axis=1), jnp.concatenate([zero, block], axis=1)], axis=0
    )


def body(
    gen_noise, renoise, gen_step, renoise_step, text_pooled, embed, mod_weight, proj_weight, unembed
):
    rows = proj_weight.shape[1]
    quarter = proj_weight.shape[2]
    fsdp_size = lax.axis_size("fsdp")
    row_start = lax.axis_index("fsdp") * rows
    col_start = lax.axis_index("mp") * quarter
    noisy_vec = condition(renoise_step, text_pooled)
    blank_vec = condition(renoise_step, jnp.zeros_like(text_pooled))
    gen_vec = condition(gen_step, text_pooled)
    teacher = jnp.dot(
        jnp.concatenate([noisy_vec, blank_vec], axis=0),
        mod_weight[1],
        preferred_element_type=jnp.float32,
    )
    local_mod = jnp.concatenate(
        [
            jnp.dot(gen_vec, mod_weight[0], preferred_element_type=jnp.float32),
            teacher[1:] + GUIDANCE * (teacher[:1] - teacher[1:]),
            jnp.dot(noisy_vec, mod_weight[2], preferred_element_type=jnp.float32),
        ],
        axis=0,
    )
    modulation = lax.all_gather(local_mod, "fsdp", axis=1, tiled=True)
    shift = lax.dynamic_slice_in_dim(modulation, row_start, rows, 1)
    gain = 1.0 + lax.dynamic_slice_in_dim(modulation, D + row_start, rows, 1)
    wide = embed.astype(jnp.float32)
    centred = wide - jnp.mean(wide, axis=2, keepdims=True)
    spread = jnp.einsum("mcd,med->mce", centred, centred, precision=HIGH) / D
    mine = lax.dynamic_slice_in_dim(centred, row_start, rows, 2)
    folded = jnp.einsum("mrk,mok->mro", proj_weight, unembed, preferred_element_type=jnp.float32)
    maps = jnp.einsum("mcr,mro->mco", mine * gain[:, None, :], folded, precision=HIGH)
    offsets = jnp.einsum("mr,mro->mo", shift, folded, precision=HIGH)
    own_cols = lax.dynamic_slice_in_dim(embed, col_start, quarter, 2)
    direct = (
        jnp.einsum("mck,mok->mco", own_cols, unembed, preferred_element_type=jnp.float32)
        / fsdp_size
    )
    total = lax.psum(jnp.concatenate([maps, direct, offsets[:, None, :]], axis=1), ("fsdp", "mp"))
    maps, direct, offsets = (total[:, :CH], total[:, CH : 2 * CH], total[:, 2 * CH :])
    halves = doubled(jnp.ones((CH, CH), jnp.float32))

    def inverse_std(values, which):
        energy = mm(values, doubled(spread[which])) * values
        return lax.rsqrt(jnp.maximum(mm(energy, halves), 0.0) + EPS_NORM)

    def predict(values, scale, which):
        offset = jnp.concatenate([offsets[which], offsets[which]], axis=1)
        return (
            mm(values, doubled(direct[which])) + scale * mm(values, doubled(maps[which])) + offset
        )

    latent = gen_noise[0].astype(jnp.bfloat16).astype(jnp.float32)
    gen_scale = inverse_std(latent, 0)
    clean_lat = predict(latent, gen_scale, 0)
    noise_level = renoise_step[0].astype(jnp.float32) / 1000.0
    noisy_lat = (1.0 - noise_level) * clean_lat + noise_level * renoise[0]
    noisy = noisy_lat.astype(jnp.bfloat16).astype(jnp.float32)
    real_out = predict(noisy, inverse_std(noisy, 1), 1)
    fake_out = predict(noisy, inverse_std(noisy, 2), 2)
    real_pred = noisy_lat - noise_level * real_out
    raw_gap = noise_level * (real_out - fake_out)
    moment = lax.dot_general(
        (gen_scale * latent).astype(jnp.bfloat16),
        raw_gap.astype(jnp.bfloat16),
        (((0,), (0,)), ((), ())),
        preferred_element_type=jnp.float32,
    )
    moment = moment[:CH, :CH] + moment[CH:, CH:]
    sums = jnp.sum(raw_gap, axis=0)
    sums = sums[:CH] + sums[CH:]
    distance = jnp.full((1, CH), jnp.sum(jnp.abs(clean_lat - real_pred)))
    reduced = lax.psum(jnp.concatenate([moment, sums[None], distance], axis=0), "fsdp")
    seq_len = 2 * gen_noise.shape[1] * fsdp_size
    gap_scale = reduced[CH + 1, 0] / (seq_len * CH) + EPS_GAP
    score_gap = raw_gap / gap_scale
    moment = reduced[: CH + 1] / (gap_scale * math.sqrt(seq_len * lax.axis_size("dp")))
    left = jnp.concatenate([mine[0] * gain[0][None], shift[:1]], axis=0)
    term = lax.dot_general(
        left, moment, (((0,), (0,)), ((), ())), precision=HIGH, preferred_element_type=jnp.float32
    )
    term = lax.psum(term, "dp")
    gen_grad = mm(term, unembed[0].astype(jnp.float32))
    return (gen_grad, score_gap[None])


def solution(mesh):
    return jax.shard_map(
        body,
        mesh=mesh,
        in_specs=(
            P("dp", "fsdp", None),
            P("dp", "fsdp", None),
            P("dp"),
            P("dp"),
            P("dp", None),
            P(),
            P(None, None, "fsdp"),
            P(None, "fsdp", "mp"),
            P(None, None, "mp"),
        ),
        out_specs=(P("fsdp", "mp"), P("dp", "fsdp", None)),
        check_vma=False,
    )
```

profile of v0, /device:TPU:32, one launch (start us, length us, event | category | flops | bytes accessed | tf_op | source)
XLA Modules:
  0.0 649.7 jit_solution(15895108352038117610)
XLA Ops:
  7.2 0.8 convert_reduce_fusion.1
  8.1 0.7 convert_element_type.74
  10.3 1.3 fusion.14
  11.7 1.3 fusion.16
  13.1 1.3 fusion.18
  14.4 23.9 %all_gather.3 = f32[3,6144]{1,0:T(4,128)S(1)} all-gather(f32[3,384]{1,0:T(4,128)S(1)} %pad_maximum_fusion.1), channel_id=1, replica_groups=mesh['mp'=4,'fsdp'=16,'dp'=4] {'fsdp'}, dimensions={1}, use_global_device_ids=true | all-gather | bytes 78336 | tf_op jit(solution)/shard_map/all_gather | solution.py:63
  38.6 1.7 convert_subtract_fusion
  40.3 0.4 fusion.140
  41.1 0.3 fusion.96
  41.4 1.4 fusion.24
  42.8 0.8 pad_maximum_fusion
  43.7 2.6 convolution_multiply_fusion.4
  46.3 1.0 fusion.66
  47.3 0.3 fusion.2
  48.0 492.4 %all-reduce.20.cloned.1.call-done = f32[3,129,64]{1,2,0:T(8,128)} async-done(((f32[3,129,64]{1,2,0:T(8,128)}), f32[3,129,64]{1,2,0:T(8,128)}) %all-reduce.20.cloned.1.call-update) | async-done | bytes 99088 | tf_op jit(solution)/shard_map/psum | solution.py:78
  540.4 0.9 slice_reduce_fusion
  541.5 1.0 slice_bitcast_fusion.2
  542.5 0.3 fusion
  542.8 0.3 fusion.28
  543.1 0.3 convolution_multiply_fusion.3
  543.7 0.3 convolution_multiply_fusion.1
  544.2 0.3 convolution_multiply_fusion.2
  544.6 0.3 convolution_multiply_fusion
  544.9 0.9 abs_reduce_fusion
  545.8 0.3 fusion.139
  546.6 0.7 pad.20.clone
  547.4 71.8 %psum.22 = f32[66,64]{0,1:T(8,128)S(1)} all-reduce(f32[66,64]{0,1:T(8,128)S(1)} %maximum_maximum_fusion), channel_id=1, replica_groups=mesh['mp'=4,'fsdp'=16,'dp'=4] {'fsdp'}, use_global_device_ids=true, to_apply=%region_4.5 | all-reduce | flops 4224 | bytes 33792 | tf_op jit(solution)/shard_map/psum | solution.py:112
  619.1 0.6 slice.142
  620.4 0.7 divide_bitcast_fusion
  621.0 0.3 fusion.33
  621.4 20.3 %psum.23 = f32[192,64]{1,0:T(8,128)S(1)} all-reduce(f32[192,64]{1,0:T(8,128)S(1)} %fusion.33), channel_id=1, replica_groups=mesh['mp'=4,'fsdp'=16,'dp'=4] {'dp'}, use_global_device_ids=true, to_apply=%region_5.6 | all-reduce | flops 12288 | bytes 98304 | tf_op jit(solution)/shard_map/psum | solution.py:121
  641.7 1.2 fusion.29
  (44 shorter events, 2.7 us)
Async XLA Ops:
  7.2 33.2 %copy-start = (bf16[3,192,768]{2,1,0:T(8,128)(2,1)S(1)}, bf16[3,192,768]{2,1,0:T(8,128)(2,1)}, u32[]{:S(2)}) copy-start(bf16[3,192,768]{2,1,0:T(8,128)(2,1)} %param.16) | copy-start | bytes 2654212
  7.2 31.2 %copy-start.1 = (bf16[3,64,3072]{2,1,0:T(8,128)(2,1)S(1)}, bf16[3,64,3072]{2,1,0:T(8,128)(2,1)}, u32[]{:S(2)}) copy-start(bf16[3,64,3072]{2,1,0:T(8,128)(2,1)} %param.14) | copy-start | bytes 3538948
  7.2 533.2 %all-reduce.20.cloned.1.call-start = ((), (), s32[]{:S(2)}) async-start(), calls=%async_computation | async-start | bytes 393216 | tf_op jit(solution)/shard_map/psum | solution.py:78
  38.4 2.0 copy-start.2
  40.7 6.5 %copy-start.5 = (f32[1,256,128]{2,1,0:T(8,128)S(1)}, f32[1,256,128]{2,1,0:T(8,128)}, u32[]{:S(2)}) copy-start(f32[1,256,128]{2,1,0:T(8,128)} %param.9) | copy-start | bytes 393220
  41.0 6.6 %copy-start.3 = (f32[128,128]{1,0:T(8,128)S(1)}, f32[128,128]{1,0:T(8,128)}, u32[]{:S(2)}) copy-start(f32[128,128]{1,0:T(8,128)} %constant.68.clone.1) | copy-start | bytes 196612
  42.8 499.9 %copy-start.4 = (f32[1,256,128]{2,1,0:T(8,128)S(1)}, f32[1,256,128]{2,1,0:T(8,128)}, u32[]{:S(2)}) copy-start(f32[1,256,128]{2,1,0:T(8,128)} %param.10) | copy-start | bytes 393220
Sparse Core Ops, SparseCore 0:
  43.8 496.5 all-reduce.19
where the time goes:
time: 650 us
  waiting for transfers between devices  492 us (76%)
  blocking collectives  116 us (18%)
  between operations  16.4 us (3%)
  matrix products  14.6 us (2%)
  other arithmetic  6.78 us (1%)
    psum x1, waiting for transfers between devices, body(): lax.psum(jnp.concatenate([maps, direct, offsets[:, None, :]], axis=1), ('...  492 us
    psum x1, blocking collectives, body(): lax.psum(jnp.concatenate([moment, sums[None], distance], axis=0), 'fsdp')  71.8 us
    all_gather x1, blocking collectives, body(): modulation = lax.all_gather(local_mod, 'fsdp', axis=1, tiled=True)  23.9 us
    psum x1, blocking collectives, body(): term = lax.psum(term, 'dp')  20.3 us
  transfers between devices with their start and end apart: 1, of which 1 were waited for; matrix products, arithmetic and copies ran while one was open for 1% of the time, Pallas kernels for 0%

commit v1 on v0

--- a/solution.py
+++ b/solution.py
@@ -75,7 +75,9 @@
         jnp.einsum("mck,mok->mco", own_cols, unembed, preferred_element_type=jnp.float32)
         / fsdp_size
     )
-    total = lax.psum(jnp.concatenate([maps, direct, offsets[:, None, :]], axis=1), ("fsdp", "mp"))
+    total = lax.psum(
+        lax.psum(jnp.concatenate([maps, direct, offsets[:, None, :]], axis=1), "mp"), "fsdp"
+    )
     maps, direct, offsets = (total[:, :CH], total[:, CH : 2 * CH], total[:, 2 * CH :])
     halves = doubled(jnp.ones((CH, CH), jnp.float32))
 

time: 650 us -> 292 us (0.45)
  waiting for transfers between devices: 492 us -> 134 us
    psum x1 -> x2, waiting for transfers between devices: 492 us -> 134 us  [the longest x1 98.4 us: body(): lax.psum(lax.psum(jnp.concatenate([maps, direct, offsets[:, None, :]], ax...]
  transfers between devices with their start and end apart: 1 -> 2, of which waited for: 1 -> 2; matrix products, arithmetic and copies ran while one was open for 1% -> 1% of each run, Pallas kernels for 0% -> 0%
where the time goes in v1:
time: 292 us
  waiting for transfers between devices  134 us (46%)
  blocking collectives  116 us (40%)
  between operations  16.4 us (6%)
  matrix products  14.6 us (5%)
  other arithmetic  6.78 us (2%)
  local copies, waits for them, and re-layouts  3.47 us (1%)
    psum x1, waiting for transfers between devices, body(): lax.psum(lax.psum(jnp.concatenate([maps, direct, offsets[:, None, :]], ax...  98.4 us
    psum x1, blocking collectives, body(): lax.psum(jnp.concatenate([moment, sums[None], distance], axis=0), 'fsdp')  72.1 us
    psum x1, waiting for transfers between devices, body(): lax.psum(jnp.concatenate([maps, direct, offsets[:, None, :]], axis=1), 'mp')  35.8 us
    all_gather x1, blocking collectives, body(): modulation = lax.all_gather(local_mod, 'fsdp', axis=1, tiled=True)  23.9 us
    psum x1, blocking collectives, body(): term = lax.psum(term, 'dp')  20.3 us
  transfers between devices with their start and end apart: 2, of which 2 were waited for; matrix products, arithmetic and copies ran while one was open for 1% of the time, Pallas kernels for 0%

profile of v1, /device:TPU:32, one launch (start us, length us, event | category | flops | bytes accessed | tf_op | source)
XLA Modules:
  0.0 291.9 jit_solution(4851510147702803754)
XLA Ops:
  7.2 0.8 convert_reduce_fusion.1
  8.1 0.7 convert_element_type.74
  10.3 1.3 fusion.14
  11.7 1.3 fusion.16
  13.1 1.3 fusion.18
  14.4 23.9 %all_gather.3 = f32[3,6144]{1,0:T(4,128)S(1)} all-gather(f32[3,384]{1,0:T(4,128)S(1)} %pad_maximum_fusion.1), channel_id=1, replica_groups=mesh['mp'=4,'fsdp'=16,'dp'=4] {'fsdp'}, dimensions={1}, use_global_device_ids=true | all-gather | bytes 78336 | tf_op jit(solution)/shard_map/all_gather | solution.py:63
  38.6 1.7 convert_subtract_fusion
  40.4 0.4 fusion.140
  41.1 0.3 fusion.96
  41.4 1.4 fusion.24
  42.8 0.8 pad_maximum_fusion
  43.7 2.6 convolution_multiply_fusion.4
  46.4 0.3 fusion.2
  46.9 1.0 fusion.66
  47.9 35.8 %all-reduce.21.cloned.1.call-done = f32[3,129,64]{1,2,0:T(8,128)} async-done(((f32[3,129,64]{1,2,0:T(8,128)}), f32[3,129,64]{1,2,0:T(8,128)}) %all-reduce.21.cloned.1.call-update) | async-done | bytes 99088 | tf_op jit(solution)/shard_map/psum | solution.py:79
  83.8 98.4 %all-reduce.23.cloned.1.call-done = f32[3,129,64]{1,2,0:T(8,128)} async-done(((f32[3,129,64]{1,2,0:T(8,128)}), f32[3,129,64]{1,2,0:T(8,128)}) %all-reduce.23.cloned.1.call-update) | async-done | bytes 99088 | tf_op jit(solution)/shard_map/psum | solution.py:78
  182.2 0.9 slice_reduce_fusion
  183.3 0.9 slice_bitcast_fusion.2
  184.2 0.3 fusion
  184.6 0.3 fusion.28
  184.9 0.3 convolution_multiply_fusion.3
  186.0 0.3 convolution_multiply_fusion.2
  186.3 0.3 convolution_multiply_fusion
  186.7 0.9 abs_reduce_fusion
  187.6 0.3 fusion.139
  188.4 0.7 pad.20.clone
  189.2 72.1 %psum.30 = f32[66,64]{0,1:T(8,128)S(1)} all-reduce(f32[66,64]{0,1:T(8,128)S(1)} %maximum_maximum_fusion), channel_id=1, replica_groups=mesh['mp'=4,'fsdp'=16,'dp'=4] {'fsdp'}, use_global_device_ids=true, to_apply=%region_5.6 | all-reduce | flops 4224 | bytes 33792 | tf_op jit(solution)/shard_map/psum | solution.py:114
  261.3 0.6 slice.142
  262.5 0.7 divide_bitcast_fusion
  263.2 0.3 fusion.33
  263.5 20.3 %psum.31 = f32[192,64]{1,0:T(8,128)S(1)} all-reduce(f32[192,64]{1,0:T(8,128)S(1)} %fusion.33), channel_id=1, replica_groups=mesh['mp'=4,'fsdp'=16,'dp'=4] {'dp'}, use_global_device_ids=true, to_apply=%region_6.7 | all-reduce | flops 12288 | bytes 98304 | tf_op jit(solution)/shard_map/psum | solution.py:123
  283.8 1.2 fusion.29
  (47 shorter events, 3.0 us)
Async XLA Ops:
  7.2 33.2 %copy-start = (bf16[3,192,768]{2,1,0:T(8,128)(2,1)S(1)}, bf16[3,192,768]{2,1,0:T(8,128)(2,1)}, u32[]{:S(2)}) copy-start(bf16[3,192,768]{2,1,0:T(8,128)(2,1)} %param.16) | copy-start | bytes 2654212
  7.2 31.2 %copy-start.1 = (bf16[3,64,3072]{2,1,0:T(8,128)(2,1)S(1)}, bf16[3,64,3072]{2,1,0:T(8,128)(2,1)}, u32[]{:S(2)}) copy-start(bf16[3,64,3072]{2,1,0:T(8,128)(2,1)} %param.14) | copy-start | bytes 3538948
  7.2 76.5 %all-reduce.21.cloned.1.call-start = ((), (), s32[]{:S(2)}) async-start(), calls=%async_computation | async-start | bytes 393216 | tf_op jit(solution)/shard_map/psum | solution.py:79
  38.4 2.0 copy-start.2
  40.8 5.6 %copy-start.5 = (f32[1,256,128]{2,1,0:T(8,128)S(1)}, f32[1,256,128]{2,1,0:T(8,128)}, u32[]{:S(2)}) copy-start(f32[1,256,128]{2,1,0:T(8,128)} %param.9) | copy-start | bytes 393220
  40.8 5.9 %copy-start.3 = (f32[128,128]{1,0:T(8,128)S(1)}, f32[128,128]{1,0:T(8,128)}, u32[]{:S(2)}) copy-start(f32[128,128]{1,0:T(8,128)} %constant.68.clone.1) | copy-start | bytes 196612
  43.6 140.9 %copy-start.4 = (f32[1,256,128]{2,1,0:T(8,128)S(1)}, f32[1,256,128]{2,1,0:T(8,128)}, u32[]{:S(2)}) copy-start(f32[1,256,128]{2,1,0:T(8,128)} %param.10) | copy-start | bytes 393220
  43.6 138.6 %all-reduce.23.cloned.1.call-start = ((), (), s32[]{:S(2)}) async-start(), calls=%async_computation.1 | async-start | bytes 393216 | tf_op jit(solution)/shard_map/psum | solution.py:78
Sparse Core Ops, SparseCore 0:
  43.8 39.9 all-reduce.20
  87.2 94.9 all-reduce.22
